TPU v7x, 128 devices: a whole 4x4x4 slice. The times are simulated.
128 devices in a mesh: seq: 16 (over x, z), tp: 8 (over y, core).
Axes of the slice: x: 4, y: 4, z: 4, core: 2. Of those that a mesh axis runs over, the one named last changes fastest.
Arguments:
- queries: bfloat16 [4096, 8192], P('seq', 'tp'), may hold values from -1000 to 1000
- states: bfloat16 [8192, 4096], P('seq', 'tp'), may hold values from -18 to 18
- state_doc: int32 [8192], replicated, may hold values from 0 to 15, as said below
- state_pos: int32 [8192], replicated, may hold values from 0 to 511, as said below
- lengths: int32 [16], replicated, may hold values from 64 to 512, as said below
- offsets: int32 [16], replicated, may hold values from 0 to 256
- key_weight: bfloat16 [4096, 8192], P(None, 'tp'), may hold values from -1 to 1
- value_weight: bfloat16 [4096, 8192], P(None, 'tp'), may hold values from -1 to 1
- context_grad: bfloat16 [4096, 8192], P('seq', 'tp'), may hold values from -6 to 6
Outputs:
- query_grad: bfloat16 [4096, 8192], P('seq', 'tp')
- key_weight_grad: bfloat16 [4096, 8192], P('seq', 'tp')
- value_weight_grad: bfloat16 [4096, 8192], P('seq', 'tp')
Inputs may be any that keep to these rules, and one draw needn't show every extreme that they name: `state_doc`: each document has exactly 512 state rows. The 512 rows held by one index of seq name any one document at most 56 times, and in every draw some device's rows name some document exactly 56 times. `state_pos`: within one document the state rows carry each position from 0 to 511 exactly once. `lengths`: some document has length 512.
All inputs are finite; a program needn't handle non-finite values.
Results may differ from a plain program's by a relative error of at most 0.017.
Values may be sent and summed in bfloat16 or wider, within the bound.
A program may use at most 128 MiB of HBM per device.

v0:
```python
import jax
import jax.numpy as jnp
from jax import lax
from jax.sharding import PartitionSpec as P

HEAD_DIM = 128


def attend(query_rows, key_rows, value_rows, grad_rows, length, offset):
    query_count = query_rows.shape[0]
    state_count = key_rows.shape[0]
    head_count = query_rows.shape[1] // HEAD_DIM
    query_heads = query_rows.reshape(query_count, head_count, HEAD_DIM)
    key_heads = key_rows.reshape(state_count, head_count, HEAD_DIM)
    value_heads = value_rows.reshape(state_count, head_count, HEAD_DIM)
    grad_heads = grad_rows.reshape(query_count, head_count, HEAD_DIM)
    score_scale = HEAD_DIM ** (-0.5)
    scores = (
        jnp.einsum("qhd,khd->hqk", query_heads, key_heads, preferred_element_type=jnp.float32)
        * score_scale
    )
    query_index = jnp.arange(query_count)
    positions = jnp.arange(state_count)
    visible = (positions[None, :] <= offset + query_index[:, None]) & (positions[None, :] < length)
    scores = jnp.where(visible[None], scores, -jnp.inf)
    row_top = jnp.max(scores, axis=-1, keepdims=True)
    weights = jnp.exp(scores - row_top)
    probabilities = weights / jnp.sum(weights, axis=-1, keepdims=True)
    probs_low = probabilities.astype(jnp.bfloat16)
    context = jnp.einsum("hqk,khd->qhd", probs_low, value_heads, preferred_element_type=jnp.float32)
    delta_rows = jnp.sum(grad_heads.astype(jnp.float32) * context, axis=-1)
    prob_grad = jnp.einsum(
        "qhd,khd->hqk", grad_heads, value_heads, preferred_element_type=jnp.float32
    )
    score_grad = (probabilities * (prob_grad - delta_rows.T[:, :, None]) * score_scale).astype(
        jnp.bfloat16
    )
    query_grad = jnp.einsum(
        "hqk,khd->qhd", score_grad, key_heads, preferred_element_type=jnp.float32
    )
    key_grad = jnp.einsum(
        "hqk,qhd->khd", score_grad, query_heads, preferred_element_type=jnp.float32
    )
    value_grad = jnp.einsum(
        "hqk,qhd->khd", probs_low, grad_heads, preferred_element_type=jnp.float32
    )
    width = query_rows.shape[1]
    return (
        query_grad.astype(jnp.bfloat16).reshape(query_count, width),
        key_grad.astype(jnp.bfloat16).reshape(state_count, width),
        value_grad.astype(jnp.bfloat16).reshape(state_count, width),
    )


def shards(
    queries, states, state_doc, state_pos, lengths, offsets, key_weight, value_weight, context_grad
):
    seq_count = lax.axis_size("seq")
    device = lax.axis_index("seq")
    row_count = states.shape[0]
    capacity = 3 * row_count // (4 * seq_count) + row_count // 16
    docs_all = state_doc.reshape(seq_count, row_count)
    positions_all = state_pos.reshape(seq_count, row_count)
    onehot = (docs_all[:, :, None] == jnp.arange(seq_count)[None, None, :]).astype(jnp.int32)
    earlier = jnp.cumsum(onehot, axis=1) - onehot
    slots_all = jnp.sum(earlier * onehot, axis=2)
    own_docs = lax.dynamic_index_in_dim(docs_all, device, 0, keepdims=False)
    own_slots = lax.dynamic_index_in_dim(slots_all, device, 0, keepdims=False)
    targets = own_docs * capacity + own_slots
    source_row = jnp.full((seq_count * capacity,), row_count, jnp.int32)
    source_row = source_row.at[targets].set(jnp.arange(row_count, dtype=jnp.int32))
    arrival_index = jnp.arange(seq_count, dtype=jnp.int32)[:, None] * capacity + slots_all
    placed = jnp.where(docs_all == device, positions_all, row_count)
    order_slot = jnp.zeros((row_count,), jnp.int32)
    order_slot = order_slot.at[placed.reshape(-1)].set(arrival_index.reshape(-1), mode="drop")
    padded = jnp.concatenate([states, jnp.zeros((1, states.shape[1]), states.dtype)], axis=0)
    arrived = lax.all_to_all(
        jnp.take(padded, source_row, axis=0), "seq", split_axis=0, concat_axis=0, tiled=True
    )
    doc_states = lax.all_gather(jnp.take(arrived, order_slot, axis=0), "tp", axis=1, tiled=True)
    key_rows = jnp.dot(doc_states, key_weight, preferred_element_type=jnp.float32).astype(
        jnp.bfloat16
    )
    value_rows = jnp.dot(doc_states, value_weight, preferred_element_type=jnp.float32).astype(
        jnp.bfloat16
    )
    length = lax.dynamic_index_in_dim(lengths, device, 0, keepdims=False)
    offset = lax.dynamic_index_in_dim(offsets, device, 0, keepdims=False)
    query_grad, key_grad, value_grad = attend(
        queries, key_rows, value_rows, context_grad, length, offset
    )
    both_grads = jnp.concatenate([key_grad, value_grad], axis=1)
    summed = lax.psum_scatter(
        lax.dot_general(
            doc_states, both_grads, (((0,), (0,)), ((), ())), preferred_element_type=jnp.float32
        ).astype(jnp.bfloat16),
        "seq",
        scatter_dimension=0,
        tiled=True,
    ).astype(jnp.float32)
    head_width = key_weight.shape[1]
    return (
        query_grad,
        summed[:, :head_width].astype(jnp.bfloat16),
        summed[:, head_width:].astype(jnp.bfloat16),
    )


def solution(mesh):
    in_specs = (
        P("seq", "tp"),
        P("seq", "tp"),
        P(),
        P(),
        P(),
        P(),
        P(None, "tp"),
        P(None, "tp"),
        P("seq", "tp"),
    )
    out_specs = (P("seq", "tp"), P("seq", "tp"), P("seq", "tp"))
    return jax.shard_map(shards, mesh=mesh, in_specs=in_specs, out_specs=out_specs, check_vma=False)
```

profile of v0, /device:TPU:1, one launch (start us, length us, event | category | flops | bytes accessed | tf_op | source)
XLA Modules:
  0.0 280.3 jit_solution(13392253341646939702)
XLA Ops:
  7.2 0.8 eq.34
  8.0 0.8 fusion.16
  8.8 18.1 %reduce-window.6 = s32[16,16,4,128]{3,1,2,0:T(8,128)S(1)} reduce-window(s32[16,16,4,128]{3,1,2,0:T(8,128)S(1)} %fusion.16, s32[]{:T(128)} %constant.34.clone.1), window={size=1x1x1x128 pad=0_0x0_0x0_0x127_0}, to_apply=%region_0.0 | reduce-window | flops 16646144 | bytes 1048580 | tf_op jit(solution)/shard_map/reduce-window
  28.1 2.4 scatter_custom_fusion.1
  30.7 3.5 %gather_fusion = bf16[896,512]{1,0:T(8,128)(2,1)S(1)} fusion(bf16[513,512]{1,0:T(8,128)(2,1)S(1)} %concatenate.6, s32[1024]{0:T(1024)S(1)} %pad_clamp_fusion.1), kind=kCustom, calls=%fused_computation | custom fusion | bytes 1838592 | tf_op jit(solution)/shard_map/jit(_take)/gather | solution.py:78
  34.2 1.1 broadcast_select_fusion
  35.4 8.5 %all-to-all-start = ((bf16[16,56,512]{2,1,0:T(8,128)(2,1)}), bf16[16,56,512]{2,1,0:T(8,128)(2,1)S(1)}, u32[]{:S(2)}, u32[]{:S(2)}) async-start(bf16[16,56,512]{2,1,0:T(8,128)(2,1)} %broadcast_select_fusion), calls=%async_computation | async-start | bytes 1835008 | tf_op jit(solution)/shard_map/all_to_all | solution.py:77
  44.1 30.4 %scatter_custom_fusion = s32[512]{0:T(512)S(1)} fusion(s32[8192]{0:T(1024)S(1)} %compare_select_fusion, s32[8192]{0:T(1024)S(1)} %bitcast.106, s32[]{:T(128)} %constant.34.clone.1), kind=kCustom, calls=%fused_computation.56 | custom fusion | bytes 2052 | tf_op jit(solution)/shard_map/scatter | solution.py:75
  74.6 2.0 gather_fusion.1
  76.6 0.9 broadcast_select_fusion.1
  80.8 31.3 %all-gather.2.cloned.1.call-done = bf16[512,4096]{1,0:T(8,128)(2,1)} async-done(((bf16[512,512]{1,0:T(8,128)(2,1)}), bf16[512,4096]{1,0:T(8,128)(2,1)}) %all-gather.2.cloned.1.call-update) | async-done | bytes 4194320 | tf_op jit(solution)/shard_map/all_gather | solution.py:80
  112.2 9.1 %convolution_convert_fusion.1 = bf16[512,1024]{1,0:T(8,128)(2,1)S(1)} fusion(bf16[512,4096]{1,0:T(8,128)(2,1)} %all-gather.2.cloned.1.call-done, bf16[4096,1024]{1,0:T(8,128)(2,1)} %param.16), kind=kOutput, calls=%fused_computation.20 | convolution fusion | flops 4295491584 | bytes 13631488 | tf_op jit(solution)/shard_map/dot_general | solution.py:84
  121.9 10.5 %convolution_convert_fusion.2 = bf16[512,1024]{1,0:T(8,128)(2,1)} fusion(bf16[512,4096]{1,0:T(8,128)(2,1)} %all-gather.2.cloned.1.call-done, bf16[4096,1024]{1,0:T(8,128)(2,1)} %param.15), kind=kOutput, calls=%fused_computation.21 | convolution fusion | flops 4295491584 | bytes 13631488 | tf_op jit(solution)/shard_map/dot_general | solution.py:81
  132.4 1.5 copy.46
  133.9 3.4 %fusion.30 = (f32[8,256]{1,0:T(8,128)S(1)}, f32[8,256,512]{1,2,0:T(8,128)}) fusion(pred[256,512]{0,1:T(8,128)(4,1)S(1)} %fusion.17, bf16[512,8,128]{0,2,1:T(8,128)(2,1)S(1)} %bitcast.95, bf16[256,8,128]{0,2,1:T(8,128)(2,1)S(1)} %bitcast.100), kind=kOutput, calls=%fused_computation.63 | convolution fusion | flops 272630272 | bytes 5906432 | tf_op jit(solution)/shard_map/sub | solution.py:27
  137.3 2.5 fusion.10
  141.2 0.8 copy-done.3
  142.1 2.2 fusion.2
  145.1 15.8 %convolution_convert_fusion = bf16[4096,2048]{1,0:T(8,128)(2,1)} fusion(bf16[512,4096]{1,0:T(8,128)(2,1)} %all-gather.2.cloned.1.call-done, bf16[512,1024]{0,1:T(8,128)(2,1)S(1)} %bitcast.103, bf16[512,1024]{0,1:T(8,128)(2,1)S(1)} %bitcast.104), kind=kOutput, calls=%fused_computation.5 | convolution fusion | flops 8602517504 | bytes 23068672 | tf_op jit(solution)/shard_map/dot_general | solution.py:94
  161.0 1.2 copy-done.1
  162.2 1.3 convolution_convert_fusion.5
  163.4 2.0 copy.40
  165.5 105.7 %reduce-scatter.2.cloned.1.call-done = bf16[256,2048]{1,0:T(8,128)(2,1)} async-done(((bf16[4096,2048]{1,0:T(8,128)(2,1)}), bf16[256,2048]{1,0:T(8,128)(2,1)}) %reduce-scatter.2.cloned.1.call-update) | async-done | bytes 1048592 | tf_op jit(solution)/shard_map/reduce_scatter | solution.py:93
  271.2 2.2 fusion.29
  (56 shorter events, 7.3 us)
Async XLA Ops:
  7.2 23.5 %copy-start.6 = (bf16[512,512]{1,0:T(8,128)(2,1)S(1)}, bf16[512,512]{1,0:T(8,128)(2,1)}, u32[]{:S(2)}) copy-start(bf16[512,512]{1,0:T(8,128)(2,1)} %param.10) | copy-start | bytes 1572868
  30.7 13.4 %copy-start.7 = (s32[8192]{0:T(1024)S(1)}, s32[8192]{0:T(1024)}, u32[]{:S(2)}) copy-start(s32[8192]{0:T(1024)} %param.11) | copy-start | bytes 98308
  30.7 13.4 %copy-start.8 = (s32[8192]{0:T(1024)S(1)}, s32[8192]{0:T(1024)}, u32[]{:S(2)}) copy-start(s32[8192]{0:T(1024)} %param.12) | copy-start | bytes 98308
  35.4 42.4 %copy-start.9 = (s32[16]{0:T(128)S(1)}, s32[16]{0:T(128)}, u32[]{:S(2)}) copy-start(s32[16]{0:T(128)} %param.14) | copy-start | bytes 196
  35.4 43.0 %copy-start.10 = (s32[16]{0:T(128)S(1)}, s32[16]{0:T(128)}, u32[]{:S(2)}) copy-start(s32[16]{0:T(128)} %param.13) | copy-start | bytes 196
  35.4 43.6 %copy-start.4 = (bf16[256,1024]{1,0:T(8,128)(2,1)S(1)}, bf16[256,1024]{1,0:T(8,128)(2,1)}, u32[]{:S(2)}) copy-start(bf16[256,1024]{1,0:T(8,128)(2,1)} %param.9) | copy-start | bytes 1572868
  35.4 39.2 %all-to-all-start = ((bf16[16,56,512]{2,1,0:T(8,128)(2,1)}), bf16[16,56,512]{2,1,0:T(8,128)(2,1)S(1)}, u32[]{:S(2)}, u32[]{:S(2)}) async-start(bf16[16,56,512]{2,1,0:T(8,128)(2,1)} %broadcast_select_fusion), calls=%async_computation | async-start | bytes 1835008 | tf_op jit(solution)/shard_map/all_to_all | solution.py:77
  43.9 35.2 %copy-start.5 = (bf16[256,1024]{1,0:T(8,128)(2,1)S(1)}, bf16[256,1024]{1,0:T(8,128)(2,1)}, u32[]{:S(2)}) copy-start(bf16[256,1024]{1,0:T(8,128)(2,1)} %param.17) | copy-start | bytes 1572868
  43.9 68.2 %all-gather.2.cloned.1.call-start = ((), (), s32[]{:S(2)}) async-start(), calls=%async_computation.2 | async-start | bytes 4718592 | tf_op jit(solution)/shard_map/all_gather | solution.py:80
  77.5 193.7 %reduce-scatter.2.cloned.1.call-start = ((), (), s32[]{:S(2)}) async-start(), calls=%async_computation.3 | async-start | bytes 17825792 | tf_op jit(solution)/shard_map/reduce_scatter | solution.py:93
  121.9 18.8 %copy-start.2 = (bf16[512,1024]{0,1:T(8,128)(2,1)}, bf16[512,1024]{0,1:T(8,128)(2,1)S(1)}, u32[]{:S(2)}) copy-start(bf16[512,1024]{0,1:T(8,128)(2,1)S(1)} %copy.48) | copy-start | bytes 3145732
  133.9 3.5 %copy-start = (bf16[512,1024]{0,1:T(8,128)(2,1)}, bf16[512,1024]{0,1:T(8,128)(2,1)S(1)}, u32[]{:S(2)}) copy-start(bf16[512,1024]{0,1:T(8,128)(2,1)S(1)} %copy.46) | copy-start | bytes 3145732
  139.9 2.2 copy-start.3
  160.9 1.2 copy-start.1
Sparse Core Ops, SparseCore 0:
  77.7 34.4 all-gather.1
  161.1 110.0 reduce-scatter.1
where the time goes:
time: 281 us; the launch traced here: 280 us
  waiting for transfers between devices  137 us (49%)
  local copies, waits for them, and re-layouts  50 us (18%)
  matrix products  44.5 us (16%)
  other arithmetic  25.5 us (9%)
  between operations  14.4 us (5%)
  starting transfers between devices  8.81 us (3%)
    reduce_scatter x1, waiting for transfers between devices, shards(): lax.psum_scatter(lax.dot_general(doc_states, both_grads, (((0,), (0,)), (...  106 us
    all_gather x1, waiting for transfers between devices, shards(): lax.all_gather(jnp.take(arrived, order_slot, axis=0), 'tp', axis=1, tiled...  31.3 us
    scatter x1, local copies, waits for them, and re-layouts, shards(): order_slot.at[placed.reshape(-1)]  30.4 us
    another operation x2, other arithmetic  18.3 us
    dot_general x1, matrix products, shards(): lax.dot_general(doc_states, both_grads, (((0,), (0,)), ((), ())), preferr...  15.8 us
    dot_general x1, matrix products, shards(): jnp.dot(doc_states, key_weight, preferred_element_type=jnp.float32)  10.5 us
    dot_general x1, matrix products, shards(): jnp.dot(doc_states, value_weight, preferred_element_type=jnp.float32)  9.14 us
    all_to_all x1, starting transfers between devices, shards(): lax.all_to_all(jnp.take(padded, source_row, axis=0), 'seq', split_axis=0,...  8.55 us
  transfers between devices with their start and end apart: 3, of which 2 were waited for; matrix products, arithmetic and copies ran while one was open for 13% of the time, Pallas kernels for 0%

commit v1 on v0

--- a/solution.py
+++ b/solution.py
@@ -77,7 +77,12 @@
     arrived = lax.all_to_all(
         jnp.take(padded, source_row, axis=0), "seq", split_axis=0, concat_axis=0, tiled=True
     )
-    doc_states = lax.all_gather(jnp.take(arrived, order_slot, axis=0), "tp", axis=1, tiled=True)
+    doc_states = jnp.concatenate(
+        lax.all_to_all(
+            jnp.stack([jnp.take(arrived, order_slot, axis=0)] * lax.axis_size("tp")), "tp", 0, 0
+        ),
+        axis=1,
+    )
     key_rows = jnp.dot(doc_states, key_weight, preferred_element_type=jnp.float32).astype(
         jnp.bfloat16
     )

time: 281 us -> 303 us (1.078)
  waiting for transfers between devices: 137 us -> 152 us
  starting transfers between devices: 8.81 us -> 14 us
    all_to_all x0 -> x1, waiting for transfers between devices: none -> 45.7 us  [shards(): lax.all_to_all(jnp.stack([jnp.take(arrived, order_slot, axis=0)] * lax.ax...]
    all_gather x1 -> x0, waiting for transfers between devices: 31.3 us -> none  [shards(): lax.all_gather(jnp.take(arrived, order_slot, axis=0), 'tp', axis=1, tiled...]
    all_to_all x0 -> x1, starting transfers between devices: none -> 5.56 us  [shards(): lax.all_to_all(jnp.stack([jnp.take(arrived, order_slot, axis=0)] * lax.ax...]
  transfers between devices with their start and end apart: 3 -> 3, of which waited for: 2 -> 2; matrix products, arithmetic and copies ran while one was open for 13% -> 12% of each run, Pallas kernels for 0% -> 0%
where the time goes in v1:
time: 303 us; the launch traced here: 302 us
  waiting for transfers between devices  152 us (50%)
  local copies, waits for them, and re-layouts  52.5 us (17%)
  matrix products  44.5 us (15%)
  other arithmetic  24.7 us (8%)
  between operations  14.4 us (5%)
  starting transfers between devices  14 us (5%)
    reduce_scatter x1, waiting for transfers between devices, shards(): lax.psum_scatter(lax.dot_general(doc_states, both_grads, (((0,), (0,)), (...  106 us
    all_to_all x1, waiting for transfers between devices, shards(): lax.all_to_all(jnp.stack([jnp.take(arrived, order_slot, axis=0)] * lax.ax...  45.7 us
    scatter x1, local copies, waits for them, and re-layouts, shards(): order_slot.at[placed.reshape(-1)]  30.4 us
    another operation x2, other arithmetic  18.3 us
    dot_general x1, matrix products, shards(): lax.dot_general(doc_states, both_grads, (((0,), (0,)), ((), ())), preferr...  15.7 us
    dot_general x1, matrix products, shards(): jnp.dot(doc_states, key_weight, preferred_element_type=jnp.float32)  10.5 us
    dot_general x1, matrix products, shards(): jnp.dot(doc_states, value_weight, preferred_element_type=jnp.float32)  9.16 us
    all_to_all x1, starting transfers between devices, shards(): lax.all_to_all(jnp.take(padded, source_row, axis=0), 'seq', split_axis=0,...  8.42 us
  transfers between devices with their start and end apart: 3, of which 2 were waited for; matrix products, arithmetic and copies ran while one was open for 12% of the time, Pallas kernels for 0%

profile of v1, /device:TPU:1, one launch (start us, length us, event | category | flops | bytes accessed | tf_op | source)
XLA Modules:
  0.0 301.9 jit_solution(1820634505876601169)
XLA Ops:
  7.2 0.8 eq.34
  8.8 18.1 %reduce-window.6 = s32[16,16,4,128]{3,1,2,0:T(8,128)S(1)} reduce-window(s32[16,16,4,128]{3,1,2,0:T(8,128)S(1)} %fusion.16, s32[]{:T(128)} %constant.34.clone.1), window={size=1x1x1x128 pad=0_0x0_0x0_0x127_0}, to_apply=%region_0.0 | reduce-window | flops 16646144 | bytes 1048580 | tf_op jit(solution)/shard_map/reduce-window
  28.1 2.4 scatter_custom_fusion.1
  30.7 3.5 %gather_fusion = bf16[896,512]{1,0:T(8,128)(2,1)S(1)} fusion(bf16[513,512]{1,0:T(8,128)(2,1)S(1)} %concatenate.6, s32[1024]{0:T(1024)S(1)} %pad_clamp_fusion.1), kind=kCustom, calls=%fused_computation | custom fusion | bytes 1838592 | tf_op jit(solution)/shard_map/jit(_take)/gather | solution.py:78
  34.2 1.1 broadcast_select_fusion
  35.4 8.4 %all-to-all-start = ((bf16[16,56,512]{2,1,0:T(8,128)(2,1)}), bf16[16,56,512]{2,1,0:T(8,128)(2,1)S(1)}, u32[]{:S(2)}, u32[]{:S(2)}) async-start(bf16[16,56,512]{2,1,0:T(8,128)(2,1)} %broadcast_select_fusion), calls=%async_computation | async-start | bytes 1835008 | tf_op jit(solution)/shard_map/all_to_all | solution.py:77
  43.9 30.4 %scatter_custom_fusion = s32[512]{0:T(512)S(1)} fusion(s32[8192]{0:T(1024)S(1)} %compare_select_fusion, s32[8192]{0:T(1024)S(1)} %bitcast.109, s32[]{:T(128)} %constant.34.clone.1), kind=kCustom, calls=%fused_computation.56 | custom fusion | bytes 2052 | tf_op jit(solution)/shard_map/scatter | solution.py:75
  74.4 2.0 gather_fusion.1
  76.8 2.3 stack.2
  79.1 5.6 %all-to-all-start.1 = ((bf16[8,512,512]{1,2,0:T(8,128)(2,1)}), bf16[8,512,512]{1,2,0:T(8,128)(2,1)}, u32[]{:S(2)}, u32[]{:S(2)}) async-start(bf16[8,512,512]{1,2,0:T(8,128)(2,1)} %stack.2), calls=%async_computation.1 | async-start | bytes 8388608 | tf_op jit(solution)/shard_map/all_to_all | solution.py:81
  87.7 45.7 %all-to-all-done.1 = bf16[8,512,512]{1,2,0:T(8,128)(2,1)} async-done(((bf16[8,512,512]{1,2,0:T(8,128)(2,1)}), bf16[8,512,512]{1,2,0:T(8,128)(2,1)}, u32[]{:S(2)}, u32[]{:S(2)}) %all-to-all-start.1) | async-done | bytes 4194336 | tf_op jit(solution)/shard_map/all_to_all | solution.py:81
  133.4 9.2 %convolution_convert_fusion.1 = bf16[512,1024]{1,0:T(8,128)(2,1)S(1)} fusion(bf16[512,4096]{0,1:T(8,128)(2,1)} %bitcast.8, bf16[4096,1024]{1,0:T(8,128)(2,1)} %param.16), kind=kOutput, calls=%fused_computation.20 | convolution fusion | flops 4295491584 | bytes 13631488 | tf_op jit(solution)/shard_map/dot_general | solution.py:89
  143.1 10.5 %convolution_convert_fusion.2 = bf16[512,1024]{1,0:T(8,128)(2,1)} fusion(bf16[512,4096]{0,1:T(8,128)(2,1)} %bitcast.8, bf16[4096,1024]{1,0:T(8,128)(2,1)} %param.15), kind=kOutput, calls=%fused_computation.21 | convolution fusion | flops 4295491584 | bytes 13631488 | tf_op jit(solution)/shard_map/dot_general | solution.py:86
  153.6 1.5 copy.47
  155.2 3.4 %fusion.30 = (f32[8,256]{1,0:T(8,128)S(1)}, f32[8,256,512]{1,2,0:T(8,128)}) fusion(pred[256,512]{0,1:T(8,128)(4,1)S(1)} %fusion.17, bf16[512,8,128]{0,2,1:T(8,128)(2,1)S(1)} %bitcast.98, bf16[256,8,128]{0,2,1:T(8,128)(2,1)S(1)} %bitcast.103), kind=kOutput, calls=%fused_computation.63 | convolution fusion | flops 272630272 | bytes 5906432 | tf_op jit(solution)/shard_map/sub | solution.py:27
  158.6 2.5 fusion.10
  162.5 0.8 copy-done.3
  163.3 2.2 fusion.2
  166.4 15.7 %convolution_convert_fusion = bf16[4096,2048]{1,0:T(8,128)(2,1)} fusion(bf16[512,4096]{0,1:T(8,128)(2,1)} %bitcast.8, bf16[512,1024]{0,1:T(8,128)(2,1)S(1)} %bitcast.106, bf16[512,1024]{0,1:T(8,128)(2,1)S(1)} %bitcast.107), kind=kOutput, calls=%fused_computation.5 | convolution fusion | flops 8602517504 | bytes 23068672 | tf_op jit(solution)/shard_map/dot_general | solution.py:99
  182.1 1.2 copy-done.1
  183.3 1.3 convolution_convert_fusion.5
  184.6 2.0 copy.41
  186.7 106.2 %reduce-scatter.2.cloned.1.call-done = bf16[256,2048]{1,0:T(8,128)(2,1)} async-done(((bf16[4096,2048]{1,0:T(8,128)(2,1)}), bf16[256,2048]{1,0:T(8,128)(2,1)}) %reduce-scatter.2.cloned.1.call-update) | async-done | bytes 1048592 | tf_op jit(solution)/shard_map/reduce_scatter | solution.py:98
  292.9 2.2 fusion.29
  (57 shorter events, 8.2 us)
Async XLA Ops:
  7.2 23.5 %copy-start.6 = (bf16[512,512]{1,0:T(8,128)(2,1)S(1)}, bf16[512,512]{1,0:T(8,128)(2,1)}, u32[]{:S(2)}) copy-start(bf16[512,512]{1,0:T(8,128)(2,1)} %param.10) | copy-start | bytes 1572868
  30.7 13.2 %copy-start.7 = (s32[8192]{0:T(1024)S(1)}, s32[8192]{0:T(1024)}, u32[]{:S(2)}) copy-start(s32[8192]{0:T(1024)} %param.11) | copy-start | bytes 98308
  30.7 13.2 %copy-start.8 = (s32[8192]{0:T(1024)S(1)}, s32[8192]{0:T(1024)}, u32[]{:S(2)}) copy-start(s32[8192]{0:T(1024)} %param.12) | copy-start | bytes 98308
  35.4 39.0 %all-to-all-start = ((bf16[16,56,512]{2,1,0:T(8,128)(2,1)}), bf16[16,56,512]{2,1,0:T(8,128)(2,1)S(1)}, u32[]{:S(2)}, u32[]{:S(2)}) async-start(bf16[16,56,512]{2,1,0:T(8,128)(2,1)} %broadcast_select_fusion), calls=%async_computation | async-start | bytes 1835008 | tf_op jit(solution)/shard_map/all_to_all | solution.py:77
  79.0 5.6 %copy-start.9 = (s32[16]{0:T(128)S(1)}, s32[16]{0:T(128)}, u32[]{:S(2)}) copy-start(s32[16]{0:T(128)} %param.14) | copy-start | bytes 196
  79.0 6.2 %copy-start.10 = (s32[16]{0:T(128)S(1)}, s32[16]{0:T(128)}, u32[]{:S(2)}) copy-start(s32[16]{0:T(128)} %param.13) | copy-start | bytes 196
  79.0 6.8 %copy-start.4 = (bf16[256,1024]{1,0:T(8,128)(2,1)S(1)}, bf16[256,1024]{1,0:T(8,128)(2,1)}, u32[]{:S(2)}) copy-start(bf16[256,1024]{1,0:T(8,128)(2,1)} %param.9) | copy-start | bytes 1572868
  79.0 7.0 %copy-start.5 = (bf16[256,1024]{1,0:T(8,128)(2,1)S(1)}, bf16[256,1024]{1,0:T(8,128)(2,1)}, u32[]{:S(2)}) copy-start(bf16[256,1024]{1,0:T(8,128)(2,1)} %param.17) | copy-start | bytes 1572868
  79.1 54.3 %all-to-all-start.1 = ((bf16[8,512,512]{1,2,0:T(8,128)(2,1)}), bf16[8,512,512]{1,2,0:T(8,128)(2,1)}, u32[]{:S(2)}, u32[]{:S(2)}) async-start(bf16[8,512,512]{1,2,0:T(8,128)(2,1)} %stack.2), calls=%async_computation.1 | async-start | bytes 8388608 | tf_op jit(solution)/shard_map/all_to_all | solution.py:81
  84.6 208.2 %reduce-scatter.2.cloned.1.call-start = ((), (), s32[]{:S(2)}) async-start(), calls=%async_computation.3 | async-start | bytes 17825792 | tf_op jit(solution)/shard_map/reduce_scatter | solution.py:98
  143.1 18.9 %copy-start.2 = (bf16[512,1024]{0,1:T(8,128)(2,1)}, bf16[512,1024]{0,1:T(8,128)(2,1)S(1)}, u32[]{:S(2)}) copy-start(bf16[512,1024]{0,1:T(8,128)(2,1)S(1)} %copy.49) | copy-start | bytes 3145732
  155.1 3.4 %copy-start = (bf16[512,1024]{0,1:T(8,128)(2,1)}, bf16[512,1024]{0,1:T(8,128)(2,1)S(1)}, u32[]{:S(2)}) copy-start(bf16[512,1024]{0,1:T(8,128)(2,1)S(1)} %copy.47) | copy-start | bytes 3145732
  161.1 2.2 copy-start.3
  182.1 1.2 copy-start.1
Sparse Core Ops, SparseCore 0:
  182.3 110.5 reduce-scatter.1
